TPU v7x, 256 devices: a whole 4x4x8 slice. The times are simulated.
256 devices in a mesh: dp: 8 (over x, z_hi), context: 32 (over y, z_lo, core).
Axes of the slice: x: 4, y: 4, z: 8 (z_hi: 2, z_lo: 4; z = z_hi * 4 + z_lo), core: 2. Of those that a mesh axis runs over, the one named last changes fastest.
Arguments:
- grad_out: bfloat16 [8, 4096, 4096], P('dp', 'context'), may hold values from -6 to 6
- attn: bfloat16 [8, 4096, 4096], P('dp', 'context'), may hold values from -0.032958984 to 0.032958984
- w_out: bfloat16 [4096, 4096], P('context'), may hold values from -0.09375 to 0.09375
Outputs:
- grad_attn: bfloat16 [8, 4096, 4096], P('dp', None, 'context')
- grad_w: bfloat16 [4096, 4096], P('context')
All inputs are finite; a program needn't handle non-finite values.
Results may differ from a plain program's by a relative error of at most 0.013.
Values may be sent and summed in bfloat16 or wider, within the bound.
No kernel may reach another device: no remote copies, remote signals or barrier semaphores. Data moves between devices by JAX's collectives and lax.ppermute only.
A program may use at most 128 MiB of HBM per device.

v0:
```python
import jax
import jax.numpy as jnp
from jax import lax
from jax.sharding import PartitionSpec as P


def accumulate(heads_view, weight_cols, block_rows):
    local_part = lax.dot_general(
        block_rows, weight_cols, (((1,), (1,)), ((), ())), preferred_element_type=jnp.float32
    )
    weight_acc = lax.dot_general(
        heads_view, block_rows, (((0,), (0,)), ((), ())), preferred_element_type=jnp.float32
    )
    return (local_part, weight_acc)


def local(grad_out, attn, w_out):
    cotangent = grad_out[0]
    activations = attn[0]
    heads_view = lax.all_to_all(activations, "context", split_axis=1, concat_axis=0, tiled=True)
    head_acc, weight_acc = accumulate(
        heads_view, w_out, lax.all_gather(cotangent, "context", axis=0, tiled=True)
    )
    weight_sum = lax.psum(weight_acc.astype(jnp.bfloat16), "dp")
    return (head_acc.astype(jnp.bfloat16)[None], weight_sum)


def solution(mesh):
    in_specs = (P("dp", "context", None), P("dp", "context", None), P("context", None))
    out_specs = (P("dp", None, "context"), P("context", None))
    return jax.shard_map(local, mesh=mesh, in_specs=in_specs, out_specs=out_specs, check_vma=False)
```

profile of v0, /device:TPU:1, one launch (start us, length us, event | category | flops | bytes accessed | tf_op | source)
XLA Modules:
  0.0 370.2 jit_solution(1322192716840169379)
XLA Ops:
  7.2 0.0 copy-start
  7.2 0.0 all-gather.3.cloned.1.call-start
  7.2 0.7 all-gather.3.cloned.1.call-update
  7.9 0.0 all-reduce.2.cloned.1.call-start
  8.0 1.6 copy.5
  9.6 45.5 %all_to_all.19 = bf16[128,32,128]{0,2,1:T(8,128)(2,1)S(1)} all-to-all(bf16[128,32,128]{0,2,1:T(8,128)(2,1)S(1)} %bitcast.20), channel_id=1, replica_groups=mesh['dp'=8,'context'=32] {'context'}, dimensions={1} | all-to-all | bytes 2097152 | tf_op jit(solution)/shard_map/all_to_all | solution.py:20
  55.1 0.7 copy.6
  55.8 154.1 %all-gather.3.cloned.1.call-done = bf16[1,4096,4096]{2,1,0:T(8,128)(2,1)} async-done(((bf16[1,128,4096]{2,1,0:T(8,128)(2,1)}), bf16[1,4096,4096]{2,1,0:T(8,128)(2,1)}) %all-gather.3.cloned.1.call-update) | async-done | bytes 33554448 | tf_op jit(solution)/shard_map/all_gather | solution.py:22
  209.9 14.0 %fusion.7 = bf16[128,4096]{1,0:T(8,128)(2,1)} fusion(bf16[4096,128]{1,0:T(8,128)(2,1)S(1)} %bitcast.18, bf16[1,4096,4096]{2,1,0:T(8,128)(2,1)} %all-gather.3.cloned.1.call-done), kind=kOutput, calls=%fused_computation.5 | convolution fusion | flops 4295491584 | bytes 35651584 | tf_op jit(solution)/shard_map/dot_general | solution.py:11
  223.9 0.0 all-reduce.2.cloned.1.call-update
  223.9 0.0 copy-done
  223.9 16.2 %fusion.10 = bf16[1,4096,128]{2,1,0:T(8,128)(2,1)} fusion(bf16[128,4096]{1,0:T(8,128)(2,1)S(1)} %copy-done, bf16[1,4096,4096]{2,1,0:T(8,128)(2,1)} %all-gather.3.cloned.1.call-done), kind=kOutput, calls=%fused_computation.6 | convolution fusion | flops 4295491584 | bytes 35651584 | tf_op jit(solution)/shard_map/dot_general | solution.py:8
  240.1 121.1 %all-reduce.2.cloned.1.call-done = bf16[128,4096]{1,0:T(8,128)(2,1)} async-done(((bf16[128,4096]{1,0:T(8,128)(2,1)}), bf16[128,4096]{1,0:T(8,128)(2,1)}) %all-reduce.2.cloned.1.call-update) | async-done | bytes 1048592 | tf_op jit(solution)/shard_map/psum | solution.py:24
  361.1 2.3 copy.8
Async XLA Ops:
  7.2 216.7 %copy-start = (bf16[128,4096]{1,0:T(8,128)(2,1)S(1)}, bf16[128,4096]{1,0:T(8,128)(2,1)}, u32[]{:S(2)}) copy-start(bf16[128,4096]{1,0:T(8,128)(2,1)} %param.5) | copy-start | bytes 3145732
  7.2 202.7 %all-gather.3.cloned.1.call-start = ((), (), s32[]{:S(2)}) async-start(), calls=%async_computation.2 | async-start | bytes 34603008 | tf_op jit(solution)/shard_map/all_gather | solution.py:22
  7.9 353.2 %all-reduce.2.cloned.1.call-start = ((), (), s32[]{:S(2)}) async-start(), calls=%async_computation.1 | async-start | bytes 2097152 | tf_op jit(solution)/shard_map/psum | solution.py:24
Sparse Core Ops, SparseCore 0:
  9.9 199.9 all-gather.2
  224.0 137.0 all-reduce.1
where the time goes:
time: 370 us
  waiting for transfers between devices  276 us (75%)
  blocking collectives  45.5 us (12%)
  matrix products  30.2 us (8%)
  between operations  14.1 us (4%)
  local copies, waits for them, and re-layouts  4.57 us (1%)
    all_gather x1, waiting for transfers between devices, local(): lax.all_gather(cotangent, 'context', axis=0, tiled=True)  154 us
    psum x1, waiting for transfers between devices, local(): weight_sum = lax.psum(weight_acc.astype(jnp.bfloat16), 'dp')  121 us
    all_to_all x1, blocking collectives, local(): lax.all_to_all(activations, 'context', split_axis=1, concat_axis=0, tiled...  45.5 us
    dot_general x1, matrix products, accumulate(): lax.dot_general(block_rows, weight_cols, (((1,), (1,)), ((), ())), prefer...  16.2 us
    dot_general x1, matrix products, accumulate(): lax.dot_general(heads_view, block_rows, (((0,), (0,)), ((), ())), preferr...  14 us
  transfers between devices with their start and end apart: 2, of which 2 were waited for; matrix products, arithmetic and copies ran while one was open for 5% of the time, Pallas kernels for 0%

commit v1 on v0

--- a/solution.py
+++ b/solution.py
@@ -19,7 +19,12 @@
     activations = attn[0]
     heads_view = lax.all_to_all(activations, "context", split_axis=1, concat_axis=0, tiled=True)
     head_acc, weight_acc = accumulate(
-        heads_view, w_out, lax.all_gather(cotangent, "context", axis=0, tiled=True)
+        heads_view,
+        w_out,
+        jnp.concatenate(
+            lax.all_to_all(jnp.stack([cotangent] * lax.axis_size("context")), "context", 0, 0),
+            axis=0,
+        ),
     )
     weight_sum = lax.psum(weight_acc.astype(jnp.bfloat16), "dp")
     return (head_acc.astype(jnp.bfloat16)[None], weight_sum)

time: 370 us -> 945 us (2.55)
  blocking collectives: 45.5 us -> 769 us
  waiting for transfers between devices: 276 us -> 116 us
  local copies, waits for them, and re-layouts: 4.57 us -> 15.8 us
    all_to_all x0 -> x1, blocking collectives: none -> 731 us  [local(): lax.all_to_all(jnp.stack([cotangent] * lax.axis_size('context')), 'contex...]
    all_gather x1 -> x0, waiting for transfers between devices: 154 us -> none  [local(): lax.all_gather(cotangent, 'context', axis=0, tiled=True)]
    another operation x0 -> x1, local copies, waits for them, and re-layouts: none -> 11.8 us  [local(): jnp.stack([cotangent] * lax.axis_size('context'))]
  transfers between devices with their start and end apart: 2 -> 1, of which waited for: 2 -> 1; matrix products, arithmetic and copies ran while one was open for 5% -> 2% of each run, Pallas kernels for 0% -> 0%
where the time goes in v1:
time: 945 us
  blocking collectives  769 us (81%)
  waiting for transfers between devices  116 us (12%)
  matrix products  30.4 us (3%)
  local copies, waits for them, and re-layouts  15.8 us (2%)
  between operations  14.1 us (1%)
    all_to_all x1, blocking collectives, local(): lax.all_to_all(jnp.stack([cotangent] * lax.axis_size('context')), 'contex...  731 us
    psum x1, waiting for transfers between devices, local(): weight_sum = lax.psum(weight_acc.astype(jnp.bfloat16), 'dp')  116 us
    all_to_all x1, blocking collectives, local(): lax.all_to_all(activations, 'context', split_axis=1, concat_axis=0, tiled...  37.9 us
  transfers between devices with their start and end apart: 1, of which 1 were waited for; matrix products, arithmetic and copies ran while one was open for 2% of the time, Pallas kernels for 0%

profile of v1, /device:TPU:1, one launch (start us, length us, event | category | flops | bytes accessed | tf_op | source)
XLA Modules:
  0.0 944.7 jit_solution(6084960373157495696)
XLA Ops:
  7.2 0.0 copy-start
  7.2 0.0 all-reduce.2.cloned.1.call-start
  7.2 1.7 copy.5
  8.9 37.9 %all_to_all.21 = bf16[128,32,128]{0,2,1:T(8,128)(2,1)S(1)} all-to-all(bf16[128,32,128]{0,2,1:T(8,128)(2,1)S(1)} %bitcast.16), channel_id=1, replica_groups=mesh['dp'=8,'context'=32] {'context'}, dimensions={1} | all-to-all | bytes 2097152 | tf_op jit(solution)/shard_map/all_to_all | solution.py:20
  46.8 11.8 %stack.3 = bf16[32,128,4096]{2,1,0:T(8,128)(2,1)} broadcast(bf16[128,4096]{1,0:T(8,128)(2,1)} %bitcast.17), dimensions={1,2} | broadcast | bytes 34603008 | tf_op jit(solution)/shard_map/stack | solution.py:25
  58.6 730.8 %all_to_all.22 = bf16[32,128,4096]{2,1,0:T(8,128)(2,1)} all-to-all(bf16[32,128,4096]{2,1,0:T(8,128)(2,1)} %stack.3), channel_id=1, replica_groups=mesh['dp'=8,'context'=32] {'context'}, dimensions={0} | all-to-all | bytes 67108864 | tf_op jit(solution)/shard_map/all_to_all | solution.py:25
  789.4 14.2 %fusion = bf16[128,4096]{1,0:T(8,128)(2,1)} fusion(bf16[32,128,4096]{2,1,0:T(8,128)(2,1)} %all_to_all.22, bf16[128,32,128]{0,2,1:T(8,128)(2,1)S(1)} %all_to_all.21), kind=kOutput, calls=%fused_computation.1 | convolution fusion | flops 4295491584 | bytes 35651584 | tf_op jit(solution)/shard_map/dot_general | solution.py:11
  803.6 0.0 all-reduce.2.cloned.1.call-update
  803.6 0.0 copy-done
  803.6 16.3 %fusion.1 = bf16[1,4096,128]{2,1,0:T(8,128)(2,1)} fusion(bf16[4096,4096]{1,0:T(8,128)(2,1)} %bitcast.15, bf16[128,4096]{1,0:T(8,128)(2,1)S(1)} %copy-done), kind=kOutput, calls=%fused_computation.3 | convolution fusion | flops 4295491584 | bytes 35651584 | tf_op jit(solution)/shard_map/dot_general | solution.py:8
  819.9 115.7 %all-reduce.2.cloned.1.call-done = bf16[128,4096]{1,0:T(8,128)(2,1)} async-done(((bf16[128,4096]{1,0:T(8,128)(2,1)}), bf16[128,4096]{1,0:T(8,128)(2,1)}) %all-reduce.2.cloned.1.call-update) | async-done | bytes 1048592 | tf_op jit(solution)/shard_map/psum | solution.py:29
  935.5 2.3 copy.7
Async XLA Ops:
  7.2 796.5 %copy-start = (bf16[128,4096]{1,0:T(8,128)(2,1)S(1)}, bf16[128,4096]{1,0:T(8,128)(2,1)}, u32[]{:S(2)}) copy-start(bf16[128,4096]{1,0:T(8,128)(2,1)} %param.5) | copy-start | bytes 3145732
  7.2 928.4 %all-reduce.2.cloned.1.call-start = ((), (), s32[]{:S(2)}) async-start(), calls=%async_computation.2 | async-start | bytes 2097152 | tf_op jit(solution)/shard_map/psum | solution.py:29
Sparse Core Ops, SparseCore 0:
  803.7 131.7 all-reduce.1
